TPU v7x, 256 devices: a whole 4x4x8 slice. The times are simulated.
256 devices in a mesh: row: 16 (over x, y_hi, core), col: 16 (over z, y_lo).
Axes of the slice: x: 4, y: 4 (y_hi: 2, y_lo: 2; y = y_hi * 2 + y_lo), z: 8, core: 2. Of those that a mesh axis runs over, the one named last changes fastest.
Arguments:
- panel_cols: bfloat16 [48, 4096, 512], P('col', 'row'), may hold values from -6 to 6
- inverses: bfloat16 [2, 256, 256], replicated, as said below
- trailing: bfloat16 [48, 4096, 4096], P(None, 'row', 'col'), may hold values from -6 to 6
Outputs:
- updated: bfloat16 [48, 4096, 4096], P(None, 'row', 'col')
Inputs may be any that keep to these rules, and one draw needn't show every extreme that they name: `inverses`: each of the two 256 x 256 matrices is lower triangular with a positive diagonal.
All inputs are finite; a program needn't handle non-finite values.
Results may differ from a plain program's by a relative error of at most 0.0063.
Values may be sent and summed in bfloat16 or wider, within the bound.
A program may use at most 128 MiB of HBM per device.

v0:
```python
import jax
import jax.numpy as jnp
from jax import lax
from jax.sharding import PartitionSpec as P


def broadcast(value, axis, source):
    kept = jnp.where(lax.axis_index(axis) == source, value, 0).astype(value.dtype)
    return lax.psum(kept, axis)


def shards(panel_cols, inverses, trailing):
    tile_size = panel_cols.shape[1]
    grid_rows = lax.axis_size("row")
    grid_cols = lax.axis_size("col")
    col_index = lax.axis_index("col")
    left_factor = jnp.einsum(
        "tak,bk->tab", panel_cols[:, :, :tile_size], inverses[0], preferred_element_type=jnp.float32
    ).astype(jnp.bfloat16)
    couple_tile = broadcast(left_factor[0], ("row", "col"), grid_cols)
    reduced = (
        panel_cols[:, :, tile_size:].astype(jnp.float32)
        - jnp.einsum("tak,bk->tab", left_factor, couple_tile, preferred_element_type=jnp.float32)
    ).astype(jnp.bfloat16)
    right_factor = jnp.einsum(
        "tak,bk->tab", reduced, inverses[1], preferred_element_type=jnp.float32
    ).astype(jnp.bfloat16)
    factored = jnp.concatenate([left_factor, right_factor], axis=2)
    root_row = (col_index + 2) % grid_rows
    source_tile = (col_index + 2) // grid_rows
    whole_panel = lax.all_gather(factored, "col", axis=0, tiled=True)
    key_tile = broadcast(
        lax.dynamic_index_in_dim(whole_panel, source_tile, 0, keepdims=False), "row", root_row
    )
    update_sum = jnp.einsum(
        "tak,bk->tab", whole_panel, key_tile, preferred_element_type=jnp.float32
    )
    return (trailing.astype(jnp.float32) - update_sum).astype(jnp.bfloat16)


def solution(mesh):
    in_specs = (P("col", "row", None), P(), P(None, "row", "col"))
    out_specs = P(None, "row", "col")
    return jax.shard_map(shards, mesh=mesh, in_specs=in_specs, out_specs=out_specs, check_vma=False)
```

profile of v0, /device:TPU:1, one launch (start us, length us, event | category | flops | bytes accessed | tf_op | source)
XLA Modules:
  0.0 691.7 jit_solution(11645885408623004183)
XLA Ops:
  6.5 0.0 all-reduce.3.cloned.1.call-start
  6.5 1.3 convolution_convert_fusion.1
  7.9 0.7 fusion.5
  8.5 0.0 all-reduce.3.cloned.1.call-update
  8.6 0.0 all-gather.2.cloned.1.call-start
  8.6 248.9 %all-reduce.3.cloned.1.call-done = bf16[256,256]{0,1:T(8,128)(2,1)} async-done(((bf16[256,256]{0,1:T(8,128)(2,1)}), bf16[256,256]{0,1:T(8,128)(2,1)}) %all-reduce.3.cloned.1.call-update) | async-done | bytes 131088 | tf_op jit(solution)/shard_map/psum | solution.py:9
  257.6 1.7 convolution_convert_fusion
  259.3 0.1 pad_maximum_fusion
  259.3 1.2 copy.6
  260.5 0.0 all-gather.2.cloned.1.call-update
  260.5 0.0 all-reduce.5.cloned.1.call-start
  260.6 264.4 %all-gather.2.cloned.1.call-done = bf16[48,256,512]{2,1,0:T(8,128)(2,1)} async-done(((bf16[3,256,512]{2,1,0:T(8,128)(2,1)}), bf16[48,256,512]{2,1,0:T(8,128)(2,1)}) %all-gather.2.cloned.1.call-update) | async-done | bytes 12582928 | tf_op jit(solution)/shard_map/all_gather | solution.py:31
  525.0 1.7 select_bitcast_fusion
  526.7 0.0 all-reduce.5.cloned.1.call-update
  526.7 145.8 %all-reduce.5.cloned.1.call-done = bf16[256,512]{1,0:T(8,128)(2,1)} async-done(((bf16[256,512]{1,0:T(8,128)(2,1)}), bf16[256,512]{1,0:T(8,128)(2,1)}) %all-reduce.5.cloned.1.call-update) | async-done | bytes 262160 | tf_op jit(solution)/shard_map/psum | solution.py:9
  672.5 12.6 %subtract_convert_fusion = bf16[48,256,256]{2,1,0:T(8,128)(2,1)} fusion(bf16[48,256,256]{2,1,0:T(8,128)(2,1)} %param.5, bf16[48,256,512]{2,1,0:T(8,128)(2,1)} %all-gather.2.cloned.1.call-done, bf16[256,512]{1,0:T(8,128)(2,1)} %all-reduce.5.cloned.1.call-done), kind=kOutput, calls=%fused_computation | convolution fusion | flops 3230662656 | bytes 25427968 | tf_op jit(solution)/shard_map/tak,bk->tab/dot_general | solution.py:35
Async XLA Ops:
  6.5 251.0 %all-reduce.3.cloned.1.call-start = ((), (), s32[]{:S(2)}) async-start(), calls=%async_computation | async-start | bytes 262144 | tf_op jit(solution)/shard_map/psum | solution.py:9
  8.6 516.4 %all-gather.2.cloned.1.call-start = ((), (), s32[]{:S(2)}) async-start(), calls=%async_computation.1 | async-start | bytes 13369344 | tf_op jit(solution)/shard_map/all_gather | solution.py:31
  260.5 412.0 %all-reduce.5.cloned.1.call-start = ((), (), s32[]{:S(2)}) async-start(), calls=%async_computation.2 | async-start | bytes 524288 | tf_op jit(solution)/shard_map/psum | solution.py:9
Sparse Core Ops, SparseCore 0:
  12.9 244.6 all-reduce.2
  260.6 264.3 all-gather.1
  527.6 144.8 all-reduce.4
where the time goes:
time: 692 us
  waiting for transfers between devices  659 us (95%)
  matrix products  15.7 us (2%)
  between operations  13.2 us (2%)
    psum x2, waiting for transfers between devices, broadcast(): return lax.psum(kept, axis)  395 us
    all_gather x1, waiting for transfers between devices, shards(): whole_panel = lax.all_gather(factored, 'col', axis=0, tiled=True)  264 us
  transfers between devices with their start and end apart: 3, of which 3 were waited for; matrix products, arithmetic and copies ran while one was open for 0% of the time, Pallas kernels for 0%

commit v1 on v0

--- a/solution.py
+++ b/solution.py
@@ -28,7 +28,8 @@
     factored = jnp.concatenate([left_factor, right_factor], axis=2)
     root_row = (col_index + 2) % grid_rows
     source_tile = (col_index + 2) // grid_rows
-    whole_panel = lax.all_gather(factored, "col", axis=0, tiled=True)
+    outgoing = jnp.stack([factored] * lax.axis_size("col"))
+    whole_panel = jnp.concatenate(lax.all_to_all(outgoing, "col", 0, 0), axis=0)
     key_tile = broadcast(
         lax.dynamic_index_in_dim(whole_panel, source_tile, 0, keepdims=False), "row", root_row
     )

time: 692 us -> 724 us (1.046)
  waiting for transfers between devices: 659 us -> 680 us
    all_to_all x0 -> x1, waiting for transfers between devices: none -> 284 us  [shards(): whole_panel = jnp.concatenate(lax.all_to_all(outgoing, 'col', 0, 0), axis=0)]
    all_gather x1 -> x0, waiting for transfers between devices: 264 us -> none  [shards(): whole_panel = lax.all_gather(factored, 'col', axis=0, tiled=True)]
where the time goes in v1:
time: 724 us
  waiting for transfers between devices  680 us (94%)
  matrix products  15.6 us (2%)
  between operations  13.5 us (2%)
    psum x2, waiting for transfers between devices, broadcast(): return lax.psum(kept, axis)  397 us
    all_to_all x1, waiting for transfers between devices, shards(): whole_panel = jnp.concatenate(lax.all_to_all(outgoing, 'col', 0, 0), axis=0)  284 us
  transfers between devices with their start and end apart: 3, of which 3 were waited for; matrix products, arithmetic and copies ran while one was open for 0% of the time, Pallas kernels for 0%

profile of v1, /device:TPU:1, one launch (start us, length us, event | category | flops | bytes accessed | tf_op | source)
XLA Modules:
  0.0 723.6 jit_solution(6813487442443535291)
XLA Ops:
  6.5 0.0 all-reduce.3.cloned.1.call-start
  6.5 1.3 convolution_convert_fusion.1
  7.9 0.7 fusion.5
  8.5 0.0 all-reduce.3.cloned.1.call-update
  8.6 249.0 %all-reduce.3.cloned.1.call-done = bf16[256,256]{0,1:T(8,128)(2,1)} async-done(((bf16[256,256]{0,1:T(8,128)(2,1)}), bf16[256,256]{0,1:T(8,128)(2,1)}) %all-reduce.3.cloned.1.call-update) | async-done | bytes 131088 | tf_op jit(solution)/shard_map/psum | solution.py:9
  257.6 1.7 convolution_convert_fusion
  259.3 0.1 pad_maximum_fusion
  259.3 0.3 copy.4
  259.6 6.0 stack.2
  265.6 5.4 all-to-all-start
  271.0 0.0 all-reduce.5.cloned.1.call-start
  271.0 283.6 %all-to-all-done = bf16[16,3,256,512]{3,2,1,0:T(8,128)(2,1)} async-done(((bf16[16,3,256,512]{3,2,1,0:T(8,128)(2,1)}), bf16[16,3,256,512]{3,2,1,0:T(8,128)(2,1)}, u32[]{:S(2)}, u32[]{:S(2)}) %all-to-all-start) | async-done | bytes 12582944 | tf_op jit(solution)/shard_map/all_to_all | solution.py:32
  554.6 1.7 select_bitcast_fusion
  556.3 0.0 all-reduce.5.cloned.1.call-update
  556.3 147.9 %all-reduce.5.cloned.1.call-done = bf16[256,512]{1,0:T(8,128)(2,1)} async-done(((bf16[256,512]{1,0:T(8,128)(2,1)}), bf16[256,512]{1,0:T(8,128)(2,1)}) %all-reduce.5.cloned.1.call-update) | async-done | bytes 262160 | tf_op jit(solution)/shard_map/psum | solution.py:9
  704.2 12.6 %subtract_convert_fusion = bf16[48,256,256]{2,1,0:T(8,128)(2,1)} fusion(bf16[48,256,256]{2,1,0:T(8,128)(2,1)} %param.5, bf16[48,256,512]{2,1,0:T(8,128)(2,1)} %bitcast.6, bf16[256,512]{1,0:T(8,128)(2,1)} %all-reduce.5.cloned.1.call-done), kind=kOutput, calls=%fused_computation | convolution fusion | flops 3230662656 | bytes 25427968 | tf_op jit(solution)/shard_map/tak,bk->tab/dot_general | solution.py:36
Async XLA Ops:
  6.5 251.0 %all-reduce.3.cloned.1.call-start = ((), (), s32[]{:S(2)}) async-start(), calls=%async_computation.1 | async-start | bytes 262144 | tf_op jit(solution)/shard_map/psum | solution.py:9
  265.6 289.0 %all-to-all-start = ((bf16[16,3,256,512]{3,2,1,0:T(8,128)(2,1)}), bf16[16,3,256,512]{3,2,1,0:T(8,128)(2,1)}, u32[]{:S(2)}, u32[]{:S(2)}) async-start(bf16[16,3,256,512]{3,2,1,0:T(8,128)(2,1)} %stack.2), calls=%async_computation | async-start | bytes 25165824 | tf_op jit(solution)/shard_map/all_to_all | solution.py:32
  271.0 433.2 %all-reduce.5.cloned.1.call-start = ((), (), s32[]{:S(2)}) async-start(), calls=%async_computation.2 | async-start | bytes 524288 | tf_op jit(solution)/shard_map/psum | solution.py:9
Sparse Core Ops, SparseCore 0:
  12.9 244.6 all-reduce.2
  556.4 147.7 all-reduce.4

commit v2 on v0

--- a/solution.py
+++ b/solution.py
@@ -6,7 +6,8 @@
 
 def broadcast(value, axis, source):
     kept = jnp.where(lax.axis_index(axis) == source, value, 0).astype(value.dtype)
-    return lax.psum(kept, axis)
+    rest_sections = lambda page, axis_id: jnp.sum(lax.all_gather(page, axis_name=axis_id), 0)
+    return rest_sections(kept, axis)
 
 
 def shards(panel_cols, inverses, trailing):

time: 692 us -> 1140 us (1.65)
  waiting for transfers between devices: 659 us -> 1090 us
  other arithmetic: 2.4 us -> 16.1 us
    all_gather x0 -> x2, waiting for transfers between devices: none -> 824 us  [broadcast(): lax.all_gather(page, axis_name=axis_id)]
    psum x2 -> x0, waiting for transfers between devices: 395 us -> none  [broadcast(): return lax.psum(kept, axis)]
    reduce_sum x0 -> x2, other arithmetic: none -> 14.3 us  [broadcast(): jnp.sum(lax.all_gather(page, axis_name=axis_id), 0)]
where the time goes in v2:
time: 1140 us
  waiting for transfers between devices  1090 us (96%)
  other arithmetic  16.1 us (1%)
  matrix products  14.4 us (1%)
  between operations  13.2 us (1%)
    all_gather x2, waiting for transfers between devices, broadcast(): lax.all_gather(page, axis_name=axis_id)  824 us
    all_gather x1, waiting for transfers between devices, shards(): whole_panel = lax.all_gather(factored, 'col', axis=0, tiled=True)  267 us
  transfers between devices with their start and end apart: 3, of which 3 were waited for; matrix products, arithmetic and copies ran while one was open for 0% of the time, Pallas kernels for 0%

profile of v2, /device:TPU:1, one launch (start us, length us, event | category | flops | bytes accessed | tf_op | source)
XLA Modules:
  0.0 1136.5 jit_solution(2214308031572921852)
XLA Ops:
  6.5 0.0 all-gather.4.cloned.1.call-start
  6.5 1.3 convolution_convert_fusion.1
  7.9 0.8 copy.5
  8.7 0.0 all-gather.4.cloned.1.call-update
  8.7 0.0 copy-start
  8.7 0.0 copy-start.1
  8.7 0.0 all-gather.6.cloned.1.call-start
  8.8 758.9 %all-gather.4.cloned.1.call-done = bf16[256,256,256]{2,1,0:T(8,128)(2,1)} async-done(((bf16[1,256,256]{2,1,0:T(8,128)(2,1)}), bf16[256,256,256]{2,1,0:T(8,128)(2,1)}) %all-gather.4.cloned.1.call-update) | async-done | bytes 33554448 | tf_op jit(solution)/shard_map/all_gather | solution.py:9
  767.6 11.5 %reduce_sum.24 = bf16[256,256]{1,0:T(8,128)(2,1)S(1)} reduce(bf16[256,256,256]{2,1,0:T(8,128)(2,1)} %all-gather.4.cloned.1.call-done, bf16[]{:T(256)} %constant.38.clone.1), dimensions={0}, to_apply=%region_0.1 | reduce | flops 16711680 | bytes 33685504 | tf_op jit(solution)/shard_map/reduce_sum | solution.py:9
  779.1 0.0 copy-done
  779.2 0.0 copy-done.1
  779.2 0.6 convolution_convert_fusion
  779.7 0.1 pad_maximum_fusion
  779.8 1.2 copy.7
  781.0 0.0 all-gather.6.cloned.1.call-update
  781.0 0.0 all-gather.8.cloned.1.call-start
  781.1 266.7 %all-gather.6.cloned.1.call-done = bf16[48,256,512]{2,1,0:T(8,128)(2,1)} async-done(((bf16[3,256,512]{2,1,0:T(8,128)(2,1)}), bf16[48,256,512]{2,1,0:T(8,128)(2,1)}) %all-gather.6.cloned.1.call-update) | async-done | bytes 12582928 | tf_op jit(solution)/shard_map/all_gather | solution.py:32
  1047.7 1.7 dynamic-slice_select_fusion
  1049.4 0.0 all-gather.8.cloned.1.call-update
  1049.4 65.1 %all-gather.8.cloned.1.call-done = bf16[16,256,512]{2,1,0:T(8,128)(2,1)} async-done(((bf16[1,256,512]{2,1,0:T(8,128)(2,1)}), bf16[16,256,512]{2,1,0:T(8,128)(2,1)}) %all-gather.8.cloned.1.call-update) | async-done | bytes 4194320 | tf_op jit(solution)/shard_map/all_gather | solution.py:9
  1114.5 2.8 reduce_sum.25
  1117.4 12.5 %subtract_convert_fusion = bf16[48,256,256]{2,1,0:T(8,128)(2,1)} fusion(bf16[48,256,256]{2,1,0:T(8,128)(2,1)} %param.5, bf16[48,256,512]{2,1,0:T(8,128)(2,1)} %all-gather.6.cloned.1.call-done, bf16[256,512]{1,0:T(8,128)(2,1)S(1)} %reduce_sum.25), kind=kOutput, calls=%fused_computation | convolution fusion | flops 3230662656 | bytes 25427968 | tf_op jit(solution)/shard_map/tak,bk->tab/dot_general | solution.py:36
  (1 shorter events, 0.0 us)
Async XLA Ops:
  6.5 761.1 %all-gather.4.cloned.1.call-start = ((), (), s32[]{:S(2)}) async-start(), calls=%async_computation | async-start | bytes 33685504 | tf_op jit(solution)/shard_map/all_gather | solution.py:9
  8.7 770.5 %copy-start = (bf16[3,256,512]{2,1,0:T(8,128)(2,1)S(1)}, bf16[3,256,512]{2,1,0:T(8,128)(2,1)}, u32[]{:S(2)}) copy-start(bf16[3,256,512]{2,1,0:T(8,128)(2,1)} %param.3) | copy-start | bytes 2359300
  8.7 770.5 %copy-start.1 = (bf16[2,256,256]{2,1,0:T(8,128)(2,1)S(1)}, bf16[2,256,256]{2,1,0:T(8,128)(2,1)}, u32[]{:S(2)}) copy-start(bf16[2,256,256]{2,1,0:T(8,128)(2,1)} %param.4) | copy-start | bytes 786436
  8.7 1039.0 %all-gather.6.cloned.1.call-start = ((), (), s32[]{:S(2)}) async-start(), calls=%async_computation.1 | async-start | bytes 13369344 | tf_op jit(solution)/shard_map/all_gather | solution.py:32
  781.0 333.5 %all-gather.8.cloned.1.call-start = ((), (), s32[]{:S(2)}) async-start(), calls=%async_computation.2 | async-start | bytes 4456448 | tf_op jit(solution)/shard_map/all_gather | solution.py:9
Sparse Core Ops, SparseCore 0:
  9.2 758.3 all-gather.3
  781.1 266.5 all-gather.5
  1050.4 64.0 all-gather.7
